TPU v7x, 256 devices: a whole 4x4x8 slice. The times are simulated.
256 devices in a mesh: slab: 32 (over y, x, z_lo), blk: 8 (over z_hi, core).
Axes of the slice: x: 4, y: 4, z: 8 (z_hi: 4, z_lo: 2; z = z_hi * 2 + z_lo), core: 2. Of those that a mesh axis runs over, the one named last changes fastest.
Arguments:
- interior: float32 [64, 512, 512], P('slab', 'blk'), may hold values from -6 to 6
- sources: float32 [64, 512, 512], P('slab', 'blk'), may hold values from -12 to 12
- absorption: float32 [64, 512, 512], P('slab', 'blk'), may hold values from 0.1 to 4
- bem_panel: bfloat16 [8192, 131072], P('blk', 'slab'), may hold values from -0.03125 to 0.03125
- incident: bfloat16 [131072, 512], P('slab'), may hold values from -160 to 160
- node_cell: int32 [131072], P('slab'), may hold values from 0 to 255
- offset: int32 [1], replicated, may hold values from 0 to 122880, as said below
Outputs:
- relaxed: float32 [64, 512, 512], P('slab', 'blk')
- boundary_flux: float32 [8192, 512], P(('blk', 'slab'))
Inputs may be any that keep to these rules, and one draw needn't show every extreme that they name: offset is a multiple of 8192; rows offset to offset + 8191 lie among the 131072 boundary nodes.
All inputs are finite; a program needn't handle non-finite values.
Results may differ from a plain program's by a relative error of at most 0.0034.
Values sent between devices are 32-bit elements; how exact they have to be, the bound alone decides.
A program may use at most 64 MiB of HBM per device.

v0:
```python
import jax
import jax.numpy as jnp
from jax import lax
from jax.sharding import PartitionSpec as P

SWEEPS = 2


omega = 0.6
center_weight = 8.0 / 3.0


def padded_2(cells, sides, width):
    for axis, dim in sides:
        count = lax.axis_size(axis)
        ends = count - 1
        head = lax.slice_in_dim(cells, 0, width, axis=dim)
        tail = lax.slice_in_dim(cells, cells.shape[dim] - width, cells.shape[dim], axis=dim)
        cells = jnp.concatenate(
            [
                lax.ppermute(tail, axis, [(i, (i + 1) % count) for i in range(ends)]),
                cells,
                lax.ppermute(head, axis, [((i + 1) % count, i) for i in range(ends)]),
            ],
            axis=dim,
        )
    return cells


def stiffness(padded):
    along_x = padded[:, :, :-2] + padded[:, :, 2:]
    middle = padded[:, :, 1:-1]
    plus_mid = along_x + middle
    plane_sum = plus_mid[:, :-2] + plus_mid[:, 1:-1] + plus_mid[:, 2:]
    total_sum = plane_sum[:-2] + plane_sum[1:-1] + plane_sum[2:]
    cross_xy = along_x[:, :-2] + along_x[:, 2:]
    corner_sum = cross_xy[:-2] + cross_xy[2:]
    face_sum = (
        along_x[1:-1, 1:-1]
        + middle[1:-1, :-2]
        + middle[1:-1, 2:]
        + middle[:-2, 1:-1]
        + middle[2:, 1:-1]
    )
    center = middle[1:-1, 1:-1]
    edge_sum = total_sum - center - face_sum - corner_sum
    return center_weight * center - edge_sum / 6.0 - corner_sum / 12.0


def sweep_once(padded, sources, absorption):
    center = padded[1:-1, 1:-1, 1:-1]
    applied = stiffness(padded) + absorption * center
    return center + omega * (sources - applied) / (center_weight + absorption)


def pad_x(values):
    return jnp.pad(values, ((0, 0), (0, 0), (1, 1)))


def per_device(interior, sources, absorption, bem_panel, incident, node_cell, offset):
    depth_z, depth_y, width_x = interior.shape
    current = interior
    for sweep_idx in range(SWEEPS):
        padded = padded_2(current, (("slab", 0), ("blk", 1)), 1)
        current = sweep_once(pad_x(padded), sources, absorption)
    slab_cols = incident.shape[0]
    own_count = slab_cols // lax.axis_size("blk")
    x_faces = jnp.stack([interior[:, :, 0], interior[:, :, width_x - 1]], axis=-1).reshape(-1)
    own_cells = lax.dynamic_slice_in_dim(node_cell, lax.axis_index("blk") * own_count, own_count, 0)
    own_trace = jnp.take(x_faces, own_cells, axis=0)
    trace = lax.all_gather(own_trace, "blk", axis=0, tiled=True)
    fields = (incident.astype(jnp.float32) + trace[:, None]).astype(jnp.bfloat16)
    wide = fields.astype(jnp.float32)
    node_total = slab_cols * lax.axis_size("slab")
    squares = lax.psum(jnp.sum(wide * wide, axis=0), "slab")
    norms = jnp.sqrt(squares / node_total + 1e-06)
    panel_rows = bem_panel.shape[0]
    first_col = lax.axis_index("slab") * slab_cols
    shift_rows = offset[0] + lax.axis_index("blk") * panel_rows - first_col
    share = panel_rows // lax.axis_size("slab")
    product = jnp.dot(bem_panel, fields, preferred_element_type=jnp.float32)
    node_pos = shift_rows + jnp.arange(panel_rows, dtype=jnp.int32)
    valid = (node_pos >= 0) & (node_pos < slab_cols)
    picked = jnp.take(wide, jnp.clip(node_pos, 0, slab_cols - 1), axis=0)
    summed = product + 0.5 * jnp.where(valid[:, None], picked, 0.0)
    summed = summed / norms[None, :]
    summed_all = lax.psum(summed, "slab")
    owned = lax.dynamic_slice_in_dim(summed_all, lax.axis_index("slab") * share, share, 0)
    return (current, owned)


def solution(mesh):
    in_specs = (
        P("slab", "blk", None),
        P("slab", "blk", None),
        P("slab", "blk", None),
        P("blk", "slab"),
        P("slab", None),
        P("slab"),
        P(),
    )
    out_specs = (P("slab", "blk", None), P(("blk", "slab"), None))
    return jax.shard_map(
        per_device, mesh=mesh, in_specs=in_specs, out_specs=out_specs, check_vma=False
    )
```

profile of v0, /device:TPU:32, one launch (start us, length us, event | category | flops | bytes accessed | tf_op | source)
XLA Modules:
  0.0 480.4 jit_solution(14701295206737365730)
XLA Ops:
  7.2 0.0 all-reduce.4.cloned.1.call-start
  7.2 1.0 fusion.47
  8.2 2.9 collective-permute-start
  11.2 2.9 collective-permute-start.1
  14.1 1.0 fusion.45
  15.7 0.1 copy.18
  15.8 0.1 copy.19
  15.9 0.1 copy.15
  16.0 0.1 reshape.43
  16.1 0.8 compare_select_fusion.2
  16.9 3.5 gather_fusion
  20.4 0.8 and_select_fusion
  21.2 17.4 %all-gather = f32[8,1,512]{2,1,0:T(1,128)S(1)} all-gather(f32[1,1,512]{2,1,0:T(1,128)S(1)} %bitcast.13), channel_id=1, replica_groups=mesh['slab'=32,'blk'=8] {'blk'}, dimensions={0}, use_global_device_ids=true | all-gather | bytes 18432 | tf_op jit(solution)/shard_map/all_gather | solution.py:71
  38.6 5.4 %multiply_reduce_fusion = (f32[512]{0:T(512)S(1)}, f32[4096,512]{1,0:T(8,128)}) fusion(f32[4096]{0:T(1024)S(1)} %bitcast.10, bf16[4096,512]{1,0:T(8,128)(2,1)} %param.11), kind=kLoop, calls=%fused_computation.2 | loop fusion | flops 12582400 | bytes 12601344 | tf_op jit(solution)/shard_map/reduce_sum | solution.py:75
  44.0 79.4 %psum.14 = f32[512]{0:T(512)S(1)} all-reduce(f32[512]{0:T(512)S(1)} %get-tuple-element.12), channel_id=1, replica_groups=mesh['slab'=32,'blk'=8] {'slab'}, use_global_device_ids=true, to_apply=%region_1.2 | all-reduce | flops 512 | bytes 4096 | tf_op jit(solution)/shard_map/psum | solution.py:75
  123.4 7.4 %gather_fusion.1 = f32[1024,512]{1,0:T(8,128)S(1)} fusion(f32[4096,512]{1,0:T(8,128)} %get-tuple-element.13, s32[1024]{0:T(1024)S(1)} %get-tuple-element.27), kind=kCustom, calls=%fused_computation.1 | custom fusion | bytes 4198400 | tf_op jit(solution)/shard_map/jit(_take)/gather | solution.py:84
  130.9 0.0 copy-start
  130.9 1.9 copy.16
  132.7 0.0 collective-permute-done
  132.8 0.0 copy-done
  132.8 0.0 collective-permute-done.1
  132.9 1.3 collective-permute-start.2
  134.2 1.3 collective-permute-start.3
  135.5 11.9 %fusion = f32[1024,512]{0,1:T(8,128)} fusion(f32[1024,512]{0,1:T(8,128)} %copy.16, bf16[1024,4096]{1,0:T(8,128)(2,1)} %param.10, f32[512]{0:T(512)S(1)} %add_sqrt_fusion, pred[1024]{0:T(1024)(128)(4,1)S(1)} %get-tuple-element.28, pred[1024]{0:T(1024)(128)(4,1)S(1)} %get-tuple-element.29, bf16[4096,512]{1,0:T(8,128)(2,1)} %param.11, f32[4096]{0:T(1024)S(1)} %bitcast.11), kind=kOutput, calls=%fused_computation.5 | convolution fusion | flops 4303880192 | bytes 16797696 | tf_op jit(solution)/shard_map/dot_general | solution.py:81
  147.4 0.0 copy-start.1
  147.4 0.0 copy-start.2
  147.4 0.0 all-reduce.4.cloned.1.call-update
  147.4 0.0 collective-permute-done.2
  147.4 0.0 collective-permute-done.3
  147.5 0.1 pad_maximum_fusion
  147.5 0.4 fusion.39
  147.9 0.2 slice_add_fusion.3
  148.1 0.2 copy-done.1
  148.4 0.1 copy-done.2
  148.4 0.3 fusion.28
  148.8 2.9 collective-permute-start.4
  151.7 4.7 collective-permute-start.5
  156.4 1.5 collective-permute-done.4
  157.9 2.7 collective-permute-done.5
  160.6 2.1 collective-permute-start.6
  162.7 1.3 collective-permute-start.7
  164.0 0.0 collective-permute-done.6
  164.0 4.8 collective-permute-done.7
  168.7 0.1 pad_maximum_fusion.1
  168.8 0.4 fusion.40
  169.2 0.1 slice_add_fusion
  169.3 0.1 slice_add_fusion.1
  169.4 1.0 fusion.13
  170.4 301.3 %all-reduce.4.cloned.1.call-done = f32[1024,512]{0,1:T(8,128)} async-done(((f32[1024,512]{0,1:T(8,128)}), f32[1024,512]{0,1:T(8,128)}) %all-reduce.4.cloned.1.call-update) | async-done | bytes 2097168 | tf_op jit(solution)/shard_map/psum | solution.py:87
  471.7 1.1 constant_dynamic-slice_fusion
  472.8 0.7 copy.17
  (11 shorter events, 0.1 us)
Async XLA Ops:
  7.2 464.6 %all-reduce.4.cloned.1.call-start = ((), (), s32[]{:S(2)}) async-start(), calls=%async_computation | async-start | bytes 4194304 | tf_op jit(solution)/shard_map/psum | solution.py:87
  8.2 124.5 %collective-permute-start = (f32[1,64,512]{2,1,0:T(8,128)S(1)}, f32[1,64,512]{2,1,0:T(8,128)S(1)}, u32[]{:S(2)}, u32[]{:S(2)}) collective-permute-start(f32[1,64,512]{2,1,0:T(8,128)S(1)} %get-tuple-element.22), channel_id=1, source_target_pairs={{0,8},{8,16},{16,24},{24,32},{32,40},{40,48},{48,56},{56,64},{64,7... | collective-permute-start | bytes 393224 | tf_op jit(solution)/shard_map/ppermute | solution.py:21
  11.2 121.7 %collective-permute-start.1 = (f32[1,64,512]{2,1,0:T(8,128)S(1)}, f32[1,64,512]{2,1,0:T(8,128)S(1)}, u32[]{:S(2)}, u32[]{:S(2)}) collective-permute-start(f32[1,64,512]{2,1,0:T(8,128)S(1)} %get-tuple-element.23), channel_id=1, source_target_pairs={{8,0},{16,8},{24,16},{32,24},{40,32},{48,40},{56,48},{64,56},{72,6... | collective-permute-start | bytes 393224 | tf_op jit(solution)/shard_map/ppermute | solution.py:23
  130.9 1.9 copy-start
  132.9 14.6 %collective-permute-start.2 = (f32[4,1,512]{2,1,0:T(1,128)S(1)}, f32[4,1,512]{2,1,0:T(1,128)S(1)}, u32[]{:S(2)}, u32[]{:S(2)}) collective-permute-start(f32[4,1,512]{2,1,0:T(1,128)S(1)} %get-tuple-element.16), channel_id=1, source_target_pairs={{0,1},{1,2},{2,3},{3,4},{4,5},{5,6},{6,7},{8,9},{9,10},{10,11},{11... | collective-permute-start | bytes 24584 | tf_op jit(solution)/shard_map/ppermute | solution.py:21
  134.2 13.3 %collective-permute-start.3 = (f32[4,1,512]{2,1,0:T(1,128)S(1)}, f32[4,1,512]{2,1,0:T(1,128)S(1)}, u32[]{:S(2)}, u32[]{:S(2)}) collective-permute-start(f32[4,1,512]{2,1,0:T(1,128)S(1)} %get-tuple-element.17), channel_id=1, source_target_pairs={{1,0},{2,1},{3,2},{4,3},{5,4},{6,5},{7,6},{9,8},{10,9},{11,10},{12... | collective-permute-start | bytes 24584 | tf_op jit(solution)/shard_map/ppermute | solution.py:23
  147.4 0.9 copy-start.1
  147.4 1.0 copy-start.2
  148.8 9.1 %collective-permute-start.4 = (f32[1,64,512]{2,1,0:T(8,128)S(1)}, f32[1,64,512]{2,1,0:T(8,128)S(1)}, u32[]{:S(2)}, u32[]{:S(2)}) collective-permute-start(f32[1,64,512]{2,1,0:T(8,128)S(1)} %get-tuple-element.20), channel_id=1, source_target_pairs={{0,8},{8,16},{16,24},{24,32},{32,40},{40,48},{48,56},{56,64},{64,7... | collective-permute-start | bytes 393224 | tf_op jit(solution)/shard_map/ppermute | solution.py:21
  151.7 8.8 %collective-permute-start.5 = (f32[1,64,512]{2,1,0:T(8,128)S(1)}, f32[1,64,512]{2,1,0:T(8,128)S(1)}, u32[]{:S(2)}, u32[]{:S(2)}) collective-permute-start(f32[1,64,512]{2,1,0:T(8,128)S(1)} %get-tuple-element.21), channel_id=1, source_target_pairs={{8,0},{16,8},{24,16},{32,24},{40,32},{48,40},{56,48},{64,56},{72,6... | collective-permute-start | bytes 393224 | tf_op jit(solution)/shard_map/ppermute | solution.py:23
  160.6 3.4 collective-permute-start.6
  162.7 6.1 %collective-permute-start.7 = (f32[4,1,512]{2,1,0:T(1,128)S(1)}, f32[4,1,512]{2,1,0:T(1,128)S(1)}, u32[]{:S(2)}, u32[]{:S(2)}) collective-permute-start(f32[4,1,512]{2,1,0:T(1,128)S(1)} %get-tuple-element.15), channel_id=1, source_target_pairs={{1,0},{2,1},{3,2},{4,3},{5,4},{6,5},{7,6},{9,8},{10,9},{11,10},{12... | collective-permute-start | bytes 24584 | tf_op jit(solution)/shard_map/ppermute | solution.py:23
Sparse Core Ops, SparseCore 0:
  147.6 324.1 all-reduce.3
where the time goes:
time: 481 us; the launch traced here: 480 us
  waiting for transfers between devices  310 us (64%)
  blocking collectives  96.8 us (20%)
  starting transfers between devices  19.4 us (4%)
  local copies, waits for them, and re-layouts  17.3 us (4%)
  between operations  15 us (3%)
  matrix products  11.9 us (2%)
  other arithmetic  9.66 us (2%)
    psum x1, waiting for transfers between devices, per_device(): summed_all = lax.psum(summed, 'slab')  301 us
    psum x1, blocking collectives, per_device(): squares = lax.psum(jnp.sum(wide * wide, axis=0), 'slab')  79.4 us
    all_gather x1, blocking collectives, per_device(): trace = lax.all_gather(own_trace, 'blk', axis=0, tiled=True)  17.4 us
    dot_general x1, matrix products, per_device(): product = jnp.dot(bem_panel, fields, preferred_element_type=jnp.float32)  11.9 us
    ppermute x4, starting transfers between devices, padded_2(): lax.ppermute(head, axis, [((i + 1) % count, i) for i in range(ends)])  10.1 us
  transfers between devices with their start and end apart: 9, of which 4 were waited for; matrix products, arithmetic and copies ran while one was open for 7% of the time, Pallas kernels for 0%

commit v1 on v0

v1 whole, which is shorter than its diff:
```python
import jax
import jax.numpy as jnp
from jax import lax
from jax.experimental import pallas as pl
from jax.experimental.pallas import tpu as pltpu
from jax.sharding import PartitionSpec as P

MESH = pl.DeviceIdType.MESH
F32 = jnp.float32
BF16 = jnp.bfloat16
OMEGA = 0.6
CENTER = 8.0 / 3.0

NSLAB, NBLK = 32, 8
NY, NX, NZ = 4, 4, 2
CHUNKS = 2
OPP, RIGHT, LEFT, OWN = 2, 1, 3, 0


def remote(src, dst, send_sem, recv_sem, device):
    return pltpu.make_async_remote_copy(
        src_ref=src,
        dst_ref=dst,
        send_sem=send_sem,
        recv_sem=recv_sem,
        device_id=device,
        device_id_type=MESH,
    )


def kernel(
    offset_ref,
    interior_ref,
    sources_ref,
    absorption_ref,
    panel_ref,
    incident_ref,
    cells_ref,
    relaxed_ref,
    flux_ref,
    grid0,
    grid1,
    src_v,
    abs_v,
    cells_v,
    inc_v,
    pan_v,
    acc,
    rx1,
    rx2,
    rx3,
    ysend,
    yrecv,
    trace,
    tmat,
    msgs,
    a2a,
    strip_sem,
    load_sem,
    s1_send,
    s1_recv,
    s2_send,
    s2_recv,
    s3_send,
    s3_recv,
    hz_send,
    hz_recv,
    hy_send,
    hy_recv,
    tr_send,
    tr_recv,
    aa_send,
    aa_recv,
):
    s = lax.axis_index("slab")
    b = lax.axis_index("blk")
    py = s // (NX * NZ)
    px = (s // NZ) % NX
    pz = s % NZ
    depth, rows, width = interior_ref.shape
    half = inc_v.shape[2] // 2
    chunk = rows // CHUNKS

    def slab_at(y, x, z):
        return ((y % NY) * NX + x % NX) * NZ + z

    loads = [
        pltpu.make_async_copy(interior_ref, grid0.at[1 : 1 + depth, 8 : 8 + rows, :], load_sem.at[0]),
        pltpu.make_async_copy(cells_ref, cells_v, load_sem.at[1]),
        pltpu.make_async_copy(incident_ref.at[:, :, 0:half], inc_v.at[:, :, 0:half], load_sem.at[2]),
        pltpu.make_async_copy(incident_ref.at[:, :, half:], inc_v.at[:, :, half:], load_sem.at[3]),
        pltpu.make_async_copy(sources_ref, src_v, load_sem.at[4]),
        pltpu.make_async_copy(absorption_ref, abs_v, load_sem.at[5]),
    ]

    def strip(dy, dx):
        yy = (py + dy) % NY
        xx = (px + dx) % NX
        return pltpu.make_async_copy(panel_ref.at[yy, xx], pan_v.at[yy, xx], strip_sem.at[dy, dx])

    order = [(0, OPP), (1, OPP), (0, RIGHT), (0, LEFT), (1, RIGHT), (1, LEFT), (0, OWN), (1, OWN)]

    def strips_of(h, step):
        return [(step, d) for d in range(4)] if h == 0 else [(d, step) for d in range(4)]

    loads[0].start()
    loads[1].start()
    loads[2].start()
    started = set()
    for n, (h, step) in enumerate(order):
        for key in strips_of(h, step):
            if key not in started:
                started.add(key)
                strip(*key).start()
        if n == 0:
            loads[3].start()
    loads[4].start()
    loads[5].start()

    barrier = pltpu.get_barrier_semaphore()

    def greet_slab(k, carry):
        pl.semaphore_signal(barrier, inc=1, device_id=((s + k) % NSLAB, b), device_id_type=MESH)
        return carry

    def greet_blk(k, carry):
        pl.semaphore_signal(barrier, inc=1, device_id=(s, (b + k) % NBLK), device_id_type=MESH)
        return carry

    lax.fori_loop(1, NSLAB, greet_slab, 0)
    lax.fori_loop(1, NBLK, greet_blk, 0)
    for ds in (1, NSLAB - 1):
        for db in (1, NBLK - 1):
            pl.semaphore_signal(
                barrier, inc=1, device_id=((s + ds) % NSLAB, (b + db) % NBLK), device_id_type=MESH
            )

    @pl.when(s == 0)
    def _():
        grid0[0, 8 : 8 + rows, :] = jnp.zeros((rows, width), F32)
        grid1[0, 8 : 8 + rows, :] = jnp.zeros((rows, width), F32)

    @pl.when(s == NSLAB - 1)
    def _():
        grid0[depth + 1, 8 : 8 + rows, :] = jnp.zeros((rows, width), F32)
        grid1[depth + 1, 8 : 8 + rows, :] = jnp.zeros((rows, width), F32)

    loads[0].wait()
    loads[1].wait()

    def pack_rows(grid, rnd, side):
        row = 8 if side == 0 else 7 + rows
        first = grid[1, row : row + 1, :]
        second = grid[2, row : row + 1, :]
        ysend[rnd, side] = jnp.concatenate([first, second, jnp.zeros((6, width), F32)], axis=0)

    pack_rows(grid0, 0, 0)
    pack_rows(grid0, 0, 1)

    low = [grid0[1 + z, 8 : 8 + rows, 0:128][:, 0:1] for z in range(depth)]
    high = [grid0[1 + z, 8 : 8 + rows, width - 128 :][:, 127:128] for z in range(depth)]
    faces = jnp.concatenate(low + high, axis=0)
    count = faces.shape[0]
    position = lax.broadcasted_iota(jnp.int32, (count, 128), 0)
    trace_rows = []
    for q in range(4):
        cell = cells_v[pl.ds(4 * b + q, 1), :]
        code = (cell & 1) * (depth * rows) + (cell // (2 * rows)) * rows + (cell // 2) % rows
        hit = position == code
        trace_rows.append(jnp.sum(jnp.where(hit, faces, 0.0), axis=0, keepdims=True))
    trace[b] = jnp.concatenate(trace_rows + [jnp.zeros((4, 128), F32)], axis=0)

    pl.semaphore_wait(barrier, NSLAB - 1 + NBLK - 1 + 4)

    up = (s + 1) % NSLAB
    down = (s + NSLAB - 1) % NSLAB

    def halo_z(grid, rnd, c, way):
        span = pl.ds(8 + c * chunk, chunk)
        if way == 0:
            return remote(
                grid.at[depth, span], grid.at[0, span], hz_send.at[rnd, c, 0], hz_recv.at[rnd, c, 0], (up, b)
            )
        return remote(
            grid.at[1, span], grid.at[depth + 1, span], hz_send.at[rnd, c, 1], hz_recv.at[rnd, c, 1], (down, b)
        )

    def halo_y(rnd, side, slot):
        target_s = (up, s, down)[slot]
        target_b = (b + NBLK - 1) % NBLK if side == 0 else (b + 1) % NBLK
        return remote(
            ysend.at[rnd, side],
            yrecv.at[rnd, side, slot],
            hy_send.at[rnd, side, slot],
            hy_recv.at[rnd, side, slot],
            (target_s, target_b),
        )

    def start_z(grid, rnd, c):
        @pl.when(s < NSLAB - 1)
        def _():
            halo_z(grid, rnd, c, 0).start()

        @pl.when(s > 0)
        def _():
            halo_z(grid, rnd, c, 1).start()

    def wait_z(grid, rnd, c):
        @pl.when(s > 0)
        def _():
            halo_z(grid, rnd, c, 0).wait_recv()

        @pl.when(s < NSLAB - 1)
        def _():
            halo_z(grid, rnd, c, 1).wait_recv()

    def drain_z(grid, rnd, c):
        @pl.when(s < NSLAB - 1)
        def _():
            halo_z(grid, rnd, c, 0).wait_send()

        @pl.when(s > 0)
        def _():
            halo_z(grid, rnd, c, 1).wait_send()

    def start_y(rnd, side):
        for slot in range(3):
            halo_y(rnd, side, slot).start()

    has_down = jnp.where(s > 0, 1.0, 0.0).astype(F32)
    has_up = jnp.where(s < NSLAB - 1, 1.0, 0.0).astype(F32)
    has_left = jnp.where(b > 0, 1.0, 0.0).astype(F32)
    has_right = jnp.where(b < NBLK - 1, 1.0, 0.0).astype(F32)

    def place_y(grid, rnd, edge):
        side = 1 - edge
        for slot in range(3):
            halo_y(rnd, side, slot).wait_recv()
        there = has_left if edge == 0 else has_right
        row = 7 if edge == 0 else 8 + rows
        grid[0, row : row + 1, :] = yrecv[rnd, side, 0, 1:2, :] * (there * has_down)
        grid[1, row : row + 1, :] = yrecv[rnd, side, 1, 0:1, :] * there
        grid[2, row : row + 1, :] = yrecv[rnd, side, 1, 1:2, :] * there
        grid[3, row : row + 1, :] = yrecv[rnd, side, 2, 0:1, :] * (there * has_up)

    def copy_trace(k):
        return remote(trace.at[b], trace.at[b], tr_send.at[k], tr_recv.at[k], (s, (b + k) % NBLK))

    def landed_trace(k):
        other = (b + NBLK - k) % NBLK
        return remote(trace.at[other], trace.at[other], tr_send.at[k], tr_recv.at[k], (s, other))

    for c in range(CHUNKS):
        start_z(grid0, 0, c)
    for k in range(1, NBLK):
        copy_trace(k).start()
    start_y(0, 0)
    start_y(0, 1)

    weight = jnp.where(2 * (offset_ref[0] // (2 * NBLK * 512)) + b // 4 == s, 0.5, 0.0).astype(F32)
    first = (py, px)
    second = (px, py)

    def at1(h, step):
        return (first[h] + step) % 4

    def at2(h, step):
        return (second[h] + step) % 4

    def dev1(h, step):
        if h == 0:
            return (slab_at(py + step, px, pz), b)
        return (slab_at(py, px + step, pz), b)

    def dev2(h, step):
        return dev1(1 - h, step)

    def stage1(h, kind):
        src, step = {
            0: (acc.at[h, at1(h, OPP), 0:2], RIGHT),
            1: (acc.at[h, at1(h, RIGHT), 2:4], RIGHT),
            2: (acc.at[h, at1(h, OPP), 2:4], LEFT),
            3: (acc.at[h, at1(h, LEFT), 0:2], LEFT),
            4: (acc.at[h, at1(h, RIGHT), 0:2], RIGHT),
            5: (acc.at[h, at1(h, LEFT), 2:4], LEFT),
        }[kind]
        return remote(src, rx1.at[h, kind], s1_send.at[h, kind], s1_recv.at[h, kind], dev1(h, step))

    def stage2(h, kind):
        base = at1(h, OWN)
        src, step = {
            0: (acc.at[h, base, at2(h, OPP), 0:32], RIGHT),
            1: (acc.at[h, base, at2(h, RIGHT), 32:64], RIGHT),
            2: (acc.at[h, base, at2(h, OPP), 32:64], LEFT),
            3: (acc.at[h, base, at2(h, LEFT), 0:32], LEFT),
            4: (acc.at[h, base, at2(h, RIGHT), 0:32], RIGHT),
            5: (acc.at[h, base, at2(h, LEFT), 32:64], LEFT),
        }[kind]
        return remote(src, rx2.at[h, kind], s2_send.at[h, kind], s2_recv.at[h, kind], dev2(h, step))

    def stage3(h):
        src = acc.at[h, at1(h, OWN), at2(h, OWN), pl.ds((1 - pz) * 32, 32)]
        return remote(src, rx3.at[h], s3_send.at[h], s3_recv.at[h], (slab_at(py, px, 1 - pz), b))

    waited = set()
    group0 = (b % 4) * 16

    def unit(h, step):
        for key in strips_of(h, step):
            if key not in waited:
                waited.add(key)
                strip(*key).wait()
        cols = slice(h * half, (h + 1) * half)
        where = at1(h, step)
        left = pan_v[where] if h == 0 else pan_v[:, where]
        left = left.reshape(256, left.shape[-1])
        right = inc_v[:, :, cols].reshape(left.shape[-1], half)
        product = jnp.dot(left, right, preferred_element_type=F32).reshape(4, 64, half)
        for i in range(4):
            group = group0 + (where * 4 + i if h == 0 else i * 4 + where)
            acc[h, where, i] = product[i] + weight * inc_v[group, :, cols].astype(F32)

    loads[2].wait()
    unit(0, OPP)
    stage1(0, 0).start()
    stage1(0, 2).start()
    loads[3].wait()
    unit(1, OPP)
    stage1(1, 0).start()
    stage1(1, 2).start()
    for h in (0, 1):
        unit(h, RIGHT)
        stage1(h, 1).start()
        unit(h, LEFT)
        stage1(h, 3).start()

    def pass_on1(h):
        stage1(h, 0).wait_recv()
        acc[h, at1(h, RIGHT), 0:2] += rx1[h, 0]
        stage1(h, 4).start()
        stage1(h, 2).wait_recv()
        acc[h, at1(h, LEFT), 2:4] += rx1[h, 2]
        stage1(h, 5).start()

    pass_on1(0)
    pass_on1(1)
    unit(0, OWN)
    unit(1, OWN)

    lane = lax.broadcasted_iota(jnp.int32, (chunk, width), 1)

    def sweep(grid, c, store):
        base = 8 + c * chunk
        for z in range(1, 1 + depth):
            def at(dz, dy):
                return grid[z + dz, base + dy : base + dy + chunk, :]

            ends = at(-1, 0) + at(1, 0)
            diagonal = (at(-1, -1) + at(1, -1)) + (at(-1, 1) + at(1, 1))
            plus = ends + (at(0, -1) + at(0, 1))
            mixed = 0.5 * diagonal + plus
            along = jnp.where(lane == 0, 0.0, pltpu.roll(mixed, 1, 1)) + jnp.where(
                lane == width - 1, 0.0, pltpu.roll(mixed, width - 1, 1)
            )
            center = at(0, 0)
            mass = abs_v[z - 1, c * chunk : (c + 1) * chunk, :]
            rhs = src_v[z - 1, c * chunk : (c + 1) * chunk, :]
            applied = CENTER * center - (diagonal + along) * (1.0 / 6.0) + mass * center
            store(z, c, center + OMEGA * (rhs - applied) / (CENTER + mass))

    def store1(z, c, value):
        grid1[z, 8 + c * chunk : 8 + (c + 1) * chunk, :] = value

    def store2(z, c, value):
        relaxed_ref[z - 1, c * chunk : (c + 1) * chunk, :] = value

    loads[4].wait()
    loads[5].wait()
    place_y(grid0, 0, 0)
    place_y(grid0, 0, 1)
    wait_z(grid0, 0, 0)
    for c in range(CHUNKS):
        if c + 1 < CHUNKS:
            wait_z(grid0, 0, c + 1)
        sweep(grid0, c, store1)
        start_z(grid1, 1, c)
        if c == 0:
            pack_rows(grid1, 1, 0)
            start_y(1, 0)
        if c == CHUNKS - 1:
            pack_rows(grid1, 1, 1)
            start_y(1, 1)

    def finish1(h):
        base = at1(h, OWN)
        for kind in (1, 3, 4, 5):
            stage1(h, kind).wait_recv()
        acc[h, base, 0:2] = acc[h, base, 0:2] + (rx1[h, 4] + rx1[h, 3])
        acc[h, base, 2:4] = acc[h, base, 2:4] + (rx1[h, 1] + rx1[h, 5])
        for kind in (0, 2, 1, 3):
            stage2(h, kind).start()

    def pass_on2(h):
        base = at1(h, OWN)
        stage2(h, 0).wait_recv()
        acc[h, base, at2(h, RIGHT), 0:32] += rx2[h, 0]
        stage2(h, 4).start()
        stage2(h, 2).wait_recv()
        acc[h, base, at2(h, LEFT), 32:64] += rx2[h, 2]
        stage2(h, 5).start()

    def finish2(h):
        base, own = at1(h, OWN), at2(h, OWN)
        for kind in (1, 3, 4, 5):
            stage2(h, kind).wait_recv()
        acc[h, base, own, 0:32] = acc[h, base, own, 0:32] + (rx2[h, 4] + rx2[h, 3])
        acc[h, base, own, 32:64] = acc[h, base, own, 32:64] + (rx2[h, 1] + rx2[h, 5])
        stage3(h).start()

    for k in range(1, NBLK):
        landed_trace(k).wait_recv()
    tmat[...] = jnp.zeros_like(tmat)
    for n in range(NBLK):
        for q in range(4):
            row = trace[n, q : q + 1, :]
            top = row.astype(BF16).astype(F32)
            place = slice((4 * n + q) * 128, (4 * n + q + 1) * 128)
            tmat[0:1, place] = top
            tmat[1:2, place] = row - top

    def square(n, total):
        columns = jnp.transpose(trace[n])
        for q in range(4):
            column = columns[:, q : q + 1]
            for part in range(2):
                wide = inc_v[n * 8 + q * 2 + part].astype(F32) + column[part * 64 : (part + 1) * 64]
                total = total + jnp.sum((wide * wide).reshape(8, 8, 2 * half), axis=0)
        return total

    squares = lax.fori_loop(0, NBLK, square, jnp.zeros((8, 2 * half), F32))
    squares = jnp.sum(squares, axis=0, keepdims=True)
    terms = tmat[...].astype(BF16)
    for y in range(4):
        reach = lax.dot_general(
            terms,
            pan_v[y].reshape(256, pan_v.shape[-1]),
            (((1,), (1,)), ((), ())),
            preferred_element_type=F32,
        )
        reach = reach[0:1] + reach[1:2]
        for m in range(2):
            block = 2 * y + m
            jump = trace[2 * (b % 4) + block // 4, block % 4 : block % 4 + 1, :]
            line = reach[:, m * 128 : (m + 1) * 128] + weight * jump
            msgs[block] = jnp.concatenate(
                [squares[:, q * 128 : (q + 1) * 128] for q in range(4)] + [line, jnp.zeros((3, 128), F32)], axis=0
            )

    def copy_sums(k):
        other = (s + k) % NSLAB
        return remote(msgs.at[other // 4], a2a.at[k], aa_send.at[k], aa_recv.at[k], (other, b))

    def start_sums(k, carry):
        copy_sums(k).start()
        return carry

    lax.fori_loop(1, NSLAB, start_sums, 0)

    finish1(0)
    finish1(1)
    pass_on2(0)
    pass_on2(1)
    finish2(0)
    finish2(1)

    place_y(grid1, 1, 0)
    place_y(grid1, 1, 1)
    wait_z(grid1, 1, 0)
    for c in range(CHUNKS):
        if c + 1 < CHUNKS:
            wait_z(grid1, 1, c + 1)
        sweep(grid1, c, store2)

    def add_sums(k, total):
        copy_sums(k).wait_recv()
        return total + a2a[k]

    total = lax.fori_loop(1, NSLAB, add_sums, msgs[s // 4])
    norms = jnp.concatenate([total[q : q + 1] for q in range(4)], axis=1)
    norms = jnp.sqrt(norms * (1.0 / (NSLAB * NBLK * 512)) + 1e-06)
    pick = lax.broadcasted_iota(jnp.int32, (32, 128), 1) == (s % 4) * 32 + lax.broadcasted_iota(
        jnp.int32, (32, 128), 0
    )
    reach = jnp.sum(jnp.where(pick, total[4:5], 0.0), axis=1, keepdims=True)
    for h in (0, 1):
        stage3(h).wait_recv()
        own = acc[h, at1(h, OWN), at2(h, OWN), pl.ds(pz * 32, 32)] + rx3[h]
        cols = slice(h * half, (h + 1) * half)
        flux_ref[:, cols] = (own + reach) / norms[:, cols]

    def drain_sums(k, carry):
        copy_sums(k).wait_send()
        return carry

    lax.fori_loop(1, NSLAB, drain_sums, 0)
    for h in (0, 1):
        for kind in range(6):
            stage1(h, kind).wait_send()
            stage2(h, kind).wait_send()
        stage3(h).wait_send()
    for k in range(1, NBLK):
        copy_trace(k).wait_send()
    for rnd, grid in ((0, grid0), (1, grid1)):
        for c in range(CHUNKS):
            drain_z(grid, rnd, c)
        for side in (0, 1):
            for slot in range(3):
                halo_y(rnd, side, slot).wait_send()


def per_device(interior, sources, absorption, bem_panel, incident, node_cell, offset):
    depth, rows, width = interior.shape
    nodes, fields = incident.shape
    panel_rows = bem_panel.shape[0]
    half = fields // 2
    anywhere = pl.BlockSpec(memory_space=pl.ANY)
    local = pl.BlockSpec(memory_space=pltpu.VMEM)
    dma = pltpu.SemaphoreType.DMA
    return pl.pallas_call(
        kernel,
        out_shape=(
            jax.ShapeDtypeStruct((depth, rows, width), F32),
            jax.ShapeDtypeStruct((panel_rows // NSLAB, fields), F32),
        ),
        in_specs=[pl.BlockSpec(memory_space=pltpu.SMEM)] + [anywhere] * 6,
        out_specs=(local, local),
        scratch_shapes=[
            pltpu.VMEM((depth + 2, rows + 16, width), F32),
            pltpu.VMEM((depth + 2, rows + 16, width), F32),
            pltpu.VMEM((depth, rows, width), F32),
            pltpu.VMEM((depth, rows, width), F32),
            pltpu.VMEM((nodes // 128, 128), jnp.int32),
            pltpu.VMEM((nodes // 64, 64, fields), BF16),
            pltpu.VMEM((4, 4, 64, nodes), BF16),
            pltpu.VMEM((2, 4, 4, 64, half), F32),
            pltpu.VMEM((2, 6, 2, 64, half), F32),
            pltpu.VMEM((2, 6, 32, half), F32),
            pltpu.VMEM((2, 32, half), F32),
            pltpu.VMEM((2, 2, 8, width), F32),
            pltpu.VMEM((2, 2, 3, 8, width), F32),
            pltpu.VMEM((NBLK, 8, 128), F32),
            pltpu.VMEM((16, nodes), F32),
            pltpu.VMEM((8, 8, 128), F32),
            pltpu.VMEM((NSLAB, 8, 128), F32),
            dma((4, 4)),
            dma((6,)),
            dma((2, 6)),
            dma((2, 6)),
            dma((2, 6)),
            dma((2, 6)),
            dma((2,)),
            dma((2,)),
            dma((2, CHUNKS, 2)),
            dma((2, CHUNKS, 2)),
            dma((2, 2, 3)),
            dma((2, 2, 3)),
            dma((NBLK,)),
            dma((NBLK,)),
            dma((NSLAB,)),
            dma((NSLAB,)),
        ],
        compiler_params=pltpu.CompilerParams(collective_id=0, has_side_effects=True),
    )(
        offset,
        interior,
        sources,
        absorption,
        bem_panel.reshape(4, 4, panel_rows // 16, nodes),
        incident.reshape(nodes // 64, 64, fields),
        node_cell.reshape(nodes // 128, 128),
    )


def solution(mesh):
    in_specs = (
        P("slab", "blk", None),
        P("slab", "blk", None),
        P("slab", "blk", None),
        P("blk", "slab"),
        P("slab", None),
        P("slab"),
        P(),
    )
    out_specs = (P("slab", "blk", None), P(("blk", "slab"), None))
    return jax.shard_map(
        per_device, mesh=mesh, in_specs=in_specs, out_specs=out_specs, check_vma=False
    )
```

time: 481 us -> 45.3 us (0.09)
  waiting for transfers between devices: 310 us -> 0 us
  blocking collectives: 96.8 us -> 0 us
  Pallas kernels: 0 us -> 40.5 us
  starting transfers between devices: 19.4 us -> 0 us
  local copies, waits for them, and re-layouts: 17.3 us -> 3.14 us
  between operations: 15 us -> 1.29 us
  matrix products: 11.9 us -> 0 us
  other arithmetic: 9.66 us -> 0 us
    psum x1 -> x0, waiting for transfers between devices: 301 us -> none  [per_device(): summed_all = lax.psum(summed, 'slab')]
    psum x1 -> x0, blocking collectives: 79.4 us -> none  [per_device(): squares = lax.psum(jnp.sum(wide * wide, axis=0), 'slab')]
    pallas_call x0 -> x1, Pallas kernels: none -> 40.5 us  [per_device(): pl.pallas_call(kernel, out_shape=(jax.ShapeDtypeStruct((depth, rows, widt...]
    ppermute x8 -> x0, starting transfers between devices: 19.4 us -> none  [the longest x4 10.1 us: padded_2(): lax.ppermute(head, axis, [((i + 1) % count, i) for i in range(ends)])]
    all_gather x1 -> x0, blocking collectives: 17.4 us -> none  [per_device(): trace = lax.all_gather(own_trace, 'blk', axis=0, tiled=True)]
    gather x3 -> x0, local copies, waits for them, and re-layouts: 12.8 us -> none  [the longest x2 9.26 us: per_device(): picked = jnp.take(wide, jnp.clip(node_pos, 0, slab_cols - 1), axis=0)]
    dot_general x1 -> x0, matrix products: 11.9 us -> none  [per_device(): product = jnp.dot(bem_panel, fields, preferred_element_type=jnp.float32)]
    ppermute x8 -> x0, waiting for transfers between devices: 8.91 us -> none  [the longest x4 7.44 us: padded_2(): lax.ppermute(head, axis, [((i + 1) % count, i) for i in range(ends)])]
  transfers between devices with their start and end apart: 9 -> 0, of which waited for: 4 -> 0; matrix products, arithmetic and copies ran while one was open for 7% -> 0% of each run, Pallas kernels for 0% -> 0%
where the time goes in v1:
time: 45.3 us; the launch traced here: 44.9 us
  Pallas kernels  40.5 us (89%)
  local copies, waits for them, and re-layouts  3.14 us (7%)
  between operations  1.29 us (3%)
    pallas_call x1, Pallas kernels, per_device(): pl.pallas_call(kernel, out_shape=(jax.ShapeDtypeStruct((depth, rows, widt...  40.5 us
    unnamed x2, local copies, waits for them, and re-layouts  3.14 us

profile of v1, /device:TPU:32, one launch (start us, length us, event | category | flops | bytes accessed | tf_op | source)
XLA Modules:
  0.0 44.9 jit_solution(4180786540121114511)
XLA Ops:
  1.3 40.5 %shard_map.86 = (f32[2,64,512]{2,1,0:T(8,128)}, f32[32,512]{1,0:T(8,128)}) custom-call(s32[1]{0:T(128)S(6)} %copy.11.offset_ref, f32[2,64,512]{2,1,0:T(8,128)} %interior_ref.1, f32[2,64,512]{2,1,0:T(8,128)} %sources_ref.1, f32[2,64,512]{2,1,0:T(8,128)} %absorption_ref.1, bf16[4,4,64,4096]{3,2,1,0:T(8,128)(2,1)} %bitcast.3, bf16[64,64,512]{2,1,0:T(8,128)(2,1)} %bitcast.4, ...), custom_call_target="tpu_custom_call" | custom-call | tf_op jit(solution)/shard_map/pallas_call | solution.py:529
  41.8 1.7 %copy.12 = f32[2,64,512]{2,1,0:T(8,128)} copy(f32[2,64,512]{2,1,0:T(8,128)} %get-tuple-element.4) | data formatting | bytes 524288
  43.4 1.5 %copy.13 = f32[32,512]{1,0:T(8,128)} copy(f32[32,512]{1,0:T(8,128)} %get-tuple-element.5) | data formatting | bytes 131072
